TPU v7x, 32 devices: a whole 2x2x4 slice. The times are simulated.
32 devices in a mesh: region: 4 (over y, x), col: 8 (over z, core).
Axes of the slice: x: 2, y: 2, z: 4, core: 2. Of those that a mesh axis runs over, the one named last changes fastest.
Arguments:
- jac: bfloat16 [256, 128], P(('region', 'col')), may hold values from -2 to 2
- dest: int32 [256, 2], P(('region', 'col')), may hold values from 0 to 3, all different within a row; in each aligned block of 8 rows (0 to 7, 8 to 15, ...) at most 6 rows name the same one
- near_pose: int32 [256, 2], P(('region', 'col')), may hold values from 0 to 255
- prior: float32 [8192], P('region'), may hold values from 0.5 to 8
Outputs:
- front_out: float32 [8192, 8192], P('region', 'col')
Inputs may be any that keep to these rules, and one draw needn't show every extreme that they name: `dest`: each row names two different regions; among the 8 rows of one device no region is named more than 6 times, and in some device's rows some region is named exactly 6 times.
All inputs are finite; a program needn't handle non-finite values.
Results may differ from a plain program's by a relative error of at most 0.00045.
Values may be sent and summed in bfloat16 or wider, within the bound.
No kernel may reach another device: no remote copies, remote signals or barrier semaphores. Data moves between devices by JAX's collectives and lax.ppermute only.
A program may use at most 320 MiB of HBM per device.

v0:
```python
import jax
import jax.numpy as jnp
from jax import lax
from jax.sharding import PartitionSpec as P

NB = 128
K_PANELS = 2


def broadcast(block, axis, owner):
    block = jnp.where(lax.axis_index(axis) == owner, block, jnp.zeros_like(block))
    return lax.psum(block, axis)


def placed(pose_pair, blocks, first_pose, pose_count):
    pose_grid = first_pose + jnp.arange(pose_count, dtype=jnp.int32)
    summed = jnp.zeros((blocks.shape[0], 8, pose_count, 8), jnp.float32)
    for endpoint in range(2):
        matches = (pose_pair[:, endpoint][:, None] == pose_grid[None, :]).astype(jnp.float32)
        summed = summed + matches[:, None, :, None] * blocks[:, endpoint][:, :, None, :]
    return summed.astype(jnp.bfloat16).reshape(blocks.shape[0] * 8, pose_count * 8)


def body(jac, dest, near_pose, prior):
    regions = lax.axis_size("region")
    columns = lax.axis_size("col")
    region_index = lax.axis_index("region")
    column_index = lax.axis_index("col")
    count_rows = jac.shape[0]
    row_block = prior.shape[0]
    front = row_block * regions
    col_block = front // columns
    region_poses = front // 8 // regions
    capacity = max(2, 3 * count_rows // regions)
    slots_out = regions * capacity
    targets = dest.reshape(-1)
    member = (targets[:, None] == jnp.arange(regions, dtype=jnp.int32)[None, :]).astype(jnp.int32)
    ranking = jnp.sum(jnp.cumsum(member, axis=0) * member, axis=1) - 1
    position = targets * capacity + ranking
    placing = (position[None, :] == jnp.arange(slots_out, dtype=jnp.int32)[:, None]).astype(
        jnp.bfloat16
    )
    copies = jnp.repeat(jac, 2, axis=0)
    labels = jnp.concatenate([near_pose // 64, near_pose % 64, dest], axis=1).astype(jnp.bfloat16)
    label_copies = jnp.repeat(labels, 2, axis=0)
    packed = (
        jnp.dot(placing, copies, preferred_element_type=jnp.float32)
        .astype(jnp.bfloat16)
        .reshape(regions, capacity, 128)
    )
    packed_labels = (
        jnp.dot(placing, label_copies, preferred_element_type=jnp.float32)
        .astype(jnp.bfloat16)
        .reshape(regions, capacity, 6)
    )
    arrived, arrived_labels = (
        lax.all_to_all(packed, "region", split_axis=0, concat_axis=0, tiled=True),
        lax.all_to_all(packed_labels, "region", split_axis=0, concat_axis=0, tiled=True),
    )
    piece_rows = lax.all_gather(arrived, "col", axis=0, tiled=True)
    piece_labels = lax.all_gather(arrived_labels, "col", axis=0, tiled=True)
    slot_count = piece_rows.shape[0] * piece_rows.shape[1]
    blocks = piece_rows.reshape(slot_count, 2, 8, 8).astype(jnp.float32)
    label_values = piece_labels.reshape(slot_count, 6).astype(jnp.int32)
    near_values = label_values[:, 0:2] * 64 + label_values[:, 2:4]
    pose_pair = label_values[:, 4:6] * region_poses + near_values
    own_rows = placed(pose_pair, blocks, region_index * region_poses, region_poses)
    own_cols = placed(pose_pair, blocks, column_index * (col_block // 8), col_block // 8)
    matrix = lax.dot_general(
        own_rows, own_cols, (((0,), (0,)), ((), ())), preferred_element_type=jnp.float32
    )
    row_global = region_index * row_block + jnp.arange(row_block, dtype=jnp.int32)
    col_global = column_index * col_block + jnp.arange(col_block, dtype=jnp.int32)
    matrix = matrix + jnp.where(row_global[:, None] == col_global[None, :], prior[:, None], 0.0)
    for panel_number in range(K_PANELS):
        low_edge = panel_number * NB
        high_edge = low_edge + NB
        owner_col = low_edge // col_block
        offset_col = low_edge - owner_col * col_block
        local_panel = lax.slice_in_dim(matrix, offset_col, offset_col + NB, axis=1)
        panel_part = broadcast(local_panel.astype(jnp.bfloat16), "col", owner_col).astype(
            local_panel.dtype
        )
        whole_panel = lax.all_gather(
            panel_part.astype(jnp.bfloat16), "region", axis=0, tiled=True
        ).astype(panel_part.dtype)
        diagonal = lax.slice_in_dim(whole_panel, low_edge, high_edge, axis=0)
        their_rows = lax.dynamic_slice_in_dim(
            whole_panel, column_index * col_block, col_block, axis=0
        )
        factor = jnp.tril(jnp.linalg.cholesky(diagonal))
        panel_cols = low_edge + jnp.arange(NB, dtype=jnp.int32)

        def finish(block_rows, global_rows):
            solved = jax.scipy.linalg.solve_triangular(factor, block_rows.T, lower=True).T
            keeping = global_rows[:, None] >= panel_cols[None, :]
            return jnp.where(keeping, solved, 0.0)

        mine = finish(panel_part, row_global)
        theirs = finish(their_rows, col_global)
        matrix = matrix - jnp.dot(mine, theirs.T, precision=lax.Precision.HIGHEST)
        with_panel = matrix.at[:, offset_col : offset_col + NB].set(mine)
        matrix = jnp.where(column_index == owner_col, with_panel, matrix)
        in_panel = (row_global >= low_edge) & (row_global < high_edge)
        right_side = col_global >= high_edge
        matrix = jnp.where(in_panel[:, None] & right_side[None, :], 0.0, matrix)
    return matrix


def solution(mesh):
    return jax.shard_map(
        body,
        mesh=mesh,
        in_specs=(
            P(("region", "col"), None),
            P(("region", "col"), None),
            P(("region", "col"), None),
            P("region"),
        ),
        out_specs=P("region", "col"),
        check_vma=False,
    )
```

profile of v0, /device:TPU:0, one launch (start us, length us, event | category | flops | bytes accessed | tf_op | source)
XLA Modules:
  0.0 640.7 jit_solution(2428502559729770655)
XLA Ops:
  10.1 5.2 all-to-all-start
  16.0 3.9 all-to-all-done
  19.9 3.2 all-to-all-start.1
  23.4 14.2 %all_gather.12 = bf16[32,6,6]{2,1,0:T(8,128)(2,1)S(1)} all-gather(bf16[4,6,6]{2,1,0:T(8,128)(2,1)S(1)} %copy.35), channel_id=1, replica_groups=mesh['region'=4,'col'=8] {'col'}, dimensions={0}, use_global_device_ids=true | all-gather | bytes 2592 | tf_op jit(solution)/shard_map/all_gather | solution.py:61
  38.9 14.0 %all_gather.13 = bf16[32,6,128]{2,1,0:T(8,128)(2,1)S(1)} all-gather(bf16[4,6,128]{2,1,0:T(8,128)(2,1)S(1)} %all-to-all-done.1), channel_id=1, replica_groups=mesh['region'=4,'col'=8] {'col'}, dimensions={0}, use_global_device_ids=true | all-gather | bytes 55296 | tf_op jit(solution)/shard_map/all_gather | solution.py:60
  53.9 43.1 %add_convert_fusion = bf16[192,8,256,8]{3,2,1,0:T(8,128)(2,1)} fusion(f32[192,8,8]{2,1,0:T(8,128)S(1)} %get-tuple-element.33, f32[192,256]{1,0:T(8,128)S(1)} %get-tuple-element.37, f32[192,8,8]{2,1,0:T(8,128)S(1)} %get-tuple-element.32, f32[192,256]{1,0:T(8,128)S(1)} %get-tuple-element.36), kind=kLoop, calls=%fused_computation | loop fusion | flops 12582912 | bytes 6782976 | tf_op jit(solution)/shard_map/convert_element_type | solution.py:21
  96.9 141.8 %convert_element_type.99 = bf16[1536,2048]{1,0:T(8,128)(2,1)} reshape(bf16[192,8,256,8]{3,2,1,0:T(8,128)(2,1)} %add_convert_fusion) | data formatting | bytes 12582912 | tf_op jit(solution)/shard_map/convert_element_type | solution.py:21
  238.7 23.6 %add_convert_fusion.1 = bf16[192,8,128,8]{3,2,1,0:T(8,128)(2,1)} fusion(f32[192,8,8]{2,1,0:T(8,128)S(1)} %get-tuple-element.33, f32[192,128]{1,0:T(8,128)S(1)} %copy-done.9, f32[192,8,8]{2,1,0:T(8,128)S(1)} %get-tuple-element.32, f32[192,128]{1,0:T(8,128)S(1)} %copy-done.8), kind=kLoop, calls=%fused_computation.1 | loop fusion | flops 6291456 | bytes 3440640 | tf_op jit(solution)/shard_map/convert_element_type | solution.py:21
  262.3 71.0 %convert_element_type.103 = bf16[1536,1024]{1,0:T(8,128)(2,1)S(1)} reshape(bf16[192,8,128,8]{3,2,1,0:T(8,128)(2,1)} %add_convert_fusion.1) | data formatting | bytes 6291456 | tf_op jit(solution)/shard_map/convert_element_type | solution.py:21
  333.3 9.5 %select_add_fusion = f32[2048,1024]{0,1:T(8,128)S(1)} fusion(f32[2048]{0:T(1024)S(1)} %copy-done.10, s32[2048]{0:T(1024)S(1)} %iota_add_fusion, s32[1024]{0:T(1024)S(1)} %iota_add_fusion.1, bf16[1536,2048]{1,0:T(8,128)(2,1)} %convert_element_type.99, bf16[1536,1024]{1,0:T(8,128)(2,1)S(1)} %convert_element_type.103), kind=kOutput, calls=%fused_computation.2 | convolution fusion | flops 6448742400 | bytes 17846272 | tf_op jit(solution)/shard_map/dot_general | solution.py:69
  342.8 3.4 copy-done.3
  347.1 58.0 %all-reduce.3.cloned.1.call-done = bf16[2048,128]{0,1:T(8,128)(2,1)} async-done(((bf16[2048,128]{0,1:T(8,128)(2,1)}), bf16[2048,128]{0,1:T(8,128)(2,1)}) %all-reduce.3.cloned.1.call-update) | async-done | bytes 524304 | tf_op jit(solution)/shard_map/psum | solution.py:12
  406.0 35.2 %all-gather.3.cloned.1.call-done = bf16[8192,128]{0,1:T(8,128)(2,1)} async-done(((bf16[2048,128]{0,1:T(8,128)(2,1)}), bf16[8192,128]{0,1:T(8,128)(2,1)}) %all-gather.3.cloned.1.call-update) | async-done | bytes 2097168 | tf_op jit(solution)/shard_map/all_gather | solution.py:84
  446.1 11.7 %cholesky.44 = f32[128,128]{1,0:T(8,128)S(1)} custom-call(f32[128,128]{1,0:T(8,128)S(1)} %fusion.25), custom_call_target="Cholesky" | custom-call | tf_op jit(solution)/shard_map/jit(cholesky)/cholesky | solution.py:91
  459.2 9.8 %custom-call.10 = f32[1,128,128]{1,2,0:T(8,128)S(1)} custom-call(f32[1,128,128]{2,1,0:T(8,128)S(1)} %fusion.18), custom_call_target="InvertDiagBlocksLowerTriangular" | custom-call | tf_op jit(solution)/shard_map/jit(_solve_triangular)/triangular_solve | solution.py:95
  471.8 9.4 %convolution_subtract_fusion.1 = f32[2048,1024]{0,1:T(8,128)S(1)} fusion(f32[2048,1024]{0,1:T(8,128)} %copy-done.3, f32[2048,128]{0,1:T(8,128)S(1)} %fusion.1, f32[1024,128]{0,1:T(8,128)S(1)} %fusion.3), kind=kOutput, calls=%fused_computation.6 | convolution fusion | flops 3223322624 | bytes 18350080 | tf_op jit(solution)/shard_map/dot_general | solution.py:101
  482.9 3.4 copy-done.2
  487.2 56.6 %all-reduce.5.cloned.1.call-done = bf16[2048,128]{0,1:T(8,128)(2,1)} async-done(((bf16[2048,128]{0,1:T(8,128)(2,1)}), bf16[2048,128]{0,1:T(8,128)(2,1)}) %all-reduce.5.cloned.1.call-update) | async-done | bytes 524304 | tf_op jit(solution)/shard_map/psum | solution.py:12
  544.6 35.3 %all-gather.5.cloned.1.call-done = bf16[8192,128]{0,1:T(8,128)(2,1)} async-done(((bf16[2048,128]{0,1:T(8,128)(2,1)}), bf16[8192,128]{0,1:T(8,128)(2,1)}) %all-gather.5.cloned.1.call-update) | async-done | bytes 2097168 | tf_op jit(solution)/shard_map/all_gather | solution.py:84
  584.7 11.7 %cholesky.55 = f32[128,128]{1,0:T(8,128)S(1)} custom-call(f32[128,128]{1,0:T(8,128)S(1)} %fusion.22), custom_call_target="Cholesky" | custom-call | tf_op jit(solution)/shard_map/jit(cholesky)/cholesky | solution.py:91
  597.8 9.8 %custom-call.12 = f32[1,128,128]{1,2,0:T(8,128)S(1)} custom-call(f32[1,128,128]{2,1,0:T(8,128)S(1)} %fusion.19), custom_call_target="InvertDiagBlocksLowerTriangular" | custom-call | tf_op jit(solution)/shard_map/jit(_solve_triangular)/triangular_solve | solution.py:95
  610.4 9.2 %convolution_subtract_fusion = f32[2048,1024]{0,1:T(8,128)S(1)} fusion(f32[2048,1024]{0,1:T(8,128)} %copy-done.2, f32[2048,128]{0,1:T(8,128)S(1)} %fusion, f32[1024,128]{0,1:T(8,128)S(1)} %fusion.2), kind=kOutput, calls=%fused_computation.5 | convolution fusion | flops 3223322624 | bytes 18350080 | tf_op jit(solution)/shard_map/dot_general | solution.py:101
  620.4 4.1 and_select_fusion.1
  624.5 9.2 %copy.43 = f32[2048,1024]{1,0:T(8,128)} copy(f32[2048,1024]{0,1:T(8,128)} %and_select_fusion.1) | data formatting | bytes 16777216 | tf_op jit(solution)/shard_map/jit(_where)/select_n | solution.py:106
  (91 shorter events, 30.6 us)
Async XLA Ops:
  6.5 8.7 %copy-start = (bf16[8,128]{1,0:T(8,128)(2,1)S(1)}, bf16[8,128]{1,0:T(8,128)(2,1)}, u32[]{:S(2)}) copy-start(bf16[8,128]{1,0:T(8,128)(2,1)} %param.13) | copy-start | bytes 6148
  10.1 9.9 %all-to-all-start = ((bf16[4,6,6]{1,2,0:T(8,128)(2,1)}), bf16[4,6,6]{1,2,0:T(8,128)(2,1)S(1)}, u32[]{:S(2)}, u32[]{:S(2)}) async-start(bf16[4,6,6]{1,2,0:T(8,128)(2,1)} %copy.34), calls=%async_computation | async-start | bytes 16384 | tf_op jit(solution)/shard_map/all_to_all | solution.py:58
  19.9 19.0 %all-to-all-start.1 = ((bf16[4,6,128]{2,1,0:T(8,128)(2,1)}), bf16[4,6,128]{2,1,0:T(8,128)(2,1)S(1)}, u32[]{:S(2)}, u32[]{:S(2)}) async-start(bf16[4,6,128]{2,1,0:T(8,128)(2,1)} %reshape.292), calls=%async_computation.1 | async-start | bytes 16384 | tf_op jit(solution)/shard_map/all_to_all | solution.py:57
  23.2 381.9 %all-reduce.3.cloned.1.call-start = ((), (), s32[]{:S(2)}) async-start(), calls=%async_computation.2 | async-start | bytes 1048576 | tf_op jit(solution)/shard_map/psum | solution.py:12
  96.9 141.8 %copy-start.8 = (f32[192,128]{1,0:T(8,128)S(1)}, f32[192,128]{1,0:T(8,128)}, u32[]{:S(2)}) copy-start(f32[192,128]{1,0:T(8,128)} %get-tuple-element.40) | copy-start | bytes 294916
  96.9 141.8 %copy-start.9 = (f32[192,128]{1,0:T(8,128)S(1)}, f32[192,128]{1,0:T(8,128)}, u32[]{:S(2)}) copy-start(f32[192,128]{1,0:T(8,128)} %get-tuple-element.41) | copy-start | bytes 294916
  262.3 71.0 %copy-start.10 = (f32[2048]{0:T(1024)S(1)}, f32[2048]{0:T(1024)}, u32[]{:S(2)}) copy-start(f32[2048]{0:T(1024)} %param.16) | copy-start | bytes 24580
  342.8 3.4 copy-start.3
  347.1 94.2 %all-gather.3.cloned.1.call-start = ((), (), s32[]{:S(2)}) async-start(), calls=%async_computation.3 | async-start | bytes 2621440 | tf_op jit(solution)/shard_map/all_gather | solution.py:84
  405.1 65.5 %copy-start.6 = (bf16[2048,128]{0,1:T(8,128)(2,1)S(1)}, bf16[2048,128]{0,1:T(8,128)(2,1)}, u32[]{:S(2)}) copy-start(bf16[2048,128]{0,1:T(8,128)(2,1)} %all-reduce.3.cloned.1.call-done) | copy-start | bytes 1572868
  405.2 138.7 %all-reduce.5.cloned.1.call-start = ((), (), s32[]{:S(2)}) async-start(), calls=%async_computation.4 | async-start | bytes 1048576 | tf_op jit(solution)/shard_map/psum | solution.py:12
  444.1 1.9 copy-start.5
  482.9 3.4 copy-start.2
  487.2 92.7 %all-gather.5.cloned.1.call-start = ((), (), s32[]{:S(2)}) async-start(), calls=%async_computation.5 | async-start | bytes 2621440 | tf_op jit(solution)/shard_map/all_gather | solution.py:84
  543.9 65.4 %copy-start.7 = (bf16[2048,128]{0,1:T(8,128)(2,1)S(1)}, bf16[2048,128]{0,1:T(8,128)(2,1)}, u32[]{:S(2)}) copy-start(bf16[2048,128]{0,1:T(8,128)(2,1)} %all-reduce.5.cloned.1.call-done) | copy-start | bytes 1572868
  582.7 1.9 copy-start.4
  620.4 13.4 %copy-start.1 = (bf16[8,128]{1,0:T(8,128)(2,1)S(1)}, bf16[8,128]{1,0:T(8,128)(2,1)}, u32[]{:S(2)}) copy-start(bf16[8,128]{1,0:T(8,128)(2,1)} %param.13) | copy-start | bytes 6148
Sparse Core Ops, SparseCore 0:
  347.2 57.9 all-reduce.2
  407.0 34.2 all-gather.2
  487.3 56.5 all-reduce.4
  545.6 34.2 all-gather.4
where the time goes:
time: 649 us; the launch traced here: 641 us
  local copies, waits for them, and re-layouts  238 us (37%)
  waiting for transfers between devices  189 us (29%)
  other arithmetic  129 us (20%)
  matrix products  33.8 us (5%)
  blocking collectives  28.2 us (4%)
  between operations  13.8 us (2%)
  starting transfers between devices  8.78 us (1%)
    convert_element_type x2, local copies, waits for them, and re-layouts, placed(): summed.astype(jnp.bfloat16).reshape(blocks.shape[0] * 8, pose_count * 8)  213 us
    psum x2, waiting for transfers between devices, broadcast(): return lax.psum(block, axis)  115 us
    all_gather x2, waiting for transfers between devices, body(): lax.all_gather(panel_part.astype(jnp.bfloat16), 'region', axis=0, tiled=T...  70.5 us
    convert_element_type x2, other arithmetic, placed(): summed.astype(jnp.bfloat16).reshape(blocks.shape[0] * 8, pose_count * 8)  66.7 us
    another operation x6, other arithmetic, body(): factor = jnp.tril(jnp.linalg.cholesky(diagonal))  24.9 us
    another operation x4, other arithmetic, finish(): jax.scipy.linalg.solve_triangular(factor, block_rows.T, lower=True)  20.9 us
    dot_general x2, matrix products, body(): matrix = matrix - jnp.dot(mine, theirs.T, precision=lax.Precision.HIGHEST)  18.5 us
    all_gather x1, blocking collectives, body(): piece_labels = lax.all_gather(arrived_labels, 'col', axis=0, tiled=True)  14.2 us
  transfers between devices with their start and end apart: 6, of which 5 were waited for; matrix products, arithmetic and copies ran while one was open for 1% of the time, Pallas kernels for 0%

commit v1 on v0

--- a/solution.py
+++ b/solution.py
@@ -5,6 +5,18 @@
 
 NB = 128
 K_PANELS = 2
+
+
+def gather_by_bits(value, axis, dim):
+    ways, here, step = (lax.axis_size(axis), lax.axis_index(axis), value.shape[dim])
+    line, have = (value, 1)
+    while have < ways:
+        line = jnp.concatenate(
+            [line, lax.ppermute(line, axis, [(d, (d - have) % ways) for d in range(ways)])],
+            axis=dim,
+        )
+        have = 2 * have
+    return jnp.roll(line, here * step, axis=dim)
 
 
 def broadcast(block, axis, owner):
@@ -81,9 +93,9 @@
         panel_part = broadcast(local_panel.astype(jnp.bfloat16), "col", owner_col).astype(
             local_panel.dtype
         )
-        whole_panel = lax.all_gather(
-            panel_part.astype(jnp.bfloat16), "region", axis=0, tiled=True
-        ).astype(panel_part.dtype)
+        whole_panel = gather_by_bits(panel_part.astype(jnp.bfloat16), "region", 0).astype(
+            panel_part.dtype
+        )
         diagonal = lax.slice_in_dim(whole_panel, low_edge, high_edge, axis=0)
         their_rows = lax.dynamic_slice_in_dim(
             whole_panel, column_index * col_block, col_block, axis=0

time: 649 us -> 653 us (level)
  waiting for transfers between devices: 189 us -> 180 us
  starting transfers between devices: 8.78 us -> 16.8 us
    all_gather x2 -> x0, waiting for transfers between devices: 70.5 us -> none  [body(): lax.all_gather(panel_part.astype(jnp.bfloat16), 'region', axis=0, tiled=T...]
    ppermute x0 -> x4, waiting for transfers between devices: none -> 59.5 us  [gather_by_bits(): lax.ppermute(line, axis, [(d, (d - have) % ways) for d in range(ways)])]
    ppermute x0 -> x4, starting transfers between devices: none -> 8.27 us  [gather_by_bits(): lax.ppermute(line, axis, [(d, (d - have) % ways) for d in range(ways)])]
  transfers between devices with their start and end apart: 6 -> 8, of which waited for: 5 -> 7; matrix products, arithmetic and copies ran while one was open for 1% -> 1% of each run, Pallas kernels for 0% -> 0%
where the time goes in v1:
time: 653 us; the launch traced here: 645 us
  local copies, waits for them, and re-layouts  237 us (36%)
  waiting for transfers between devices  180 us (28%)
  other arithmetic  135 us (21%)
  matrix products  33.8 us (5%)
  blocking collectives  28.2 us (4%)
  starting transfers between devices  16.8 us (3%)
  between operations  14 us (2%)
    convert_element_type x2, local copies, waits for them, and re-layouts, placed(): summed.astype(jnp.bfloat16).reshape(blocks.shape[0] * 8, pose_count * 8)  213 us
    psum x2, waiting for transfers between devices, broadcast(): return lax.psum(block, axis)  117 us
    convert_element_type x2, other arithmetic, placed(): summed.astype(jnp.bfloat16).reshape(blocks.shape[0] * 8, pose_count * 8)  66.7 us
    ppermute x4, waiting for transfers between devices, gather_by_bits(): lax.ppermute(line, axis, [(d, (d - have) % ways) for d in range(ways)])  59.5 us
    another operation x6, other arithmetic, body(): factor = jnp.tril(jnp.linalg.cholesky(diagonal))  24.9 us
    another operation x4, other arithmetic, finish(): jax.scipy.linalg.solve_triangular(factor, block_rows.T, lower=True)  21 us
    dot_general x2, matrix products, body(): matrix = matrix - jnp.dot(mine, theirs.T, precision=lax.Precision.HIGHEST)  18.5 us
    all_gather x1, blocking collectives, body(): piece_labels = lax.all_gather(arrived_labels, 'col', axis=0, tiled=True)  14.2 us
  transfers between devices with their start and end apart: 8, of which 7 were waited for; matrix products, arithmetic and copies ran while one was open for 1% of the time, Pallas kernels for 0%

profile of v1, /device:TPU:0, one launch (start us, length us, event | category | flops | bytes accessed | tf_op | source)
XLA Modules:
  0.0 644.7 jit_solution(12703639742497361199)
XLA Ops:
  10.1 5.2 all-to-all-start
  16.0 3.9 all-to-all-done
  23.4 14.2 %all_gather.6 = bf16[32,6,6]{2,1,0:T(8,128)(2,1)S(1)} all-gather(bf16[4,6,6]{2,1,0:T(8,128)(2,1)S(1)} %copy.35), channel_id=1, replica_groups=mesh['region'=4,'col'=8] {'col'}, dimensions={0}, use_global_device_ids=true | all-gather | bytes 2592 | tf_op jit(solution)/shard_map/all_gather | solution.py:73
  38.9 14.0 %all_gather.7 = bf16[32,6,128]{2,1,0:T(8,128)(2,1)S(1)} all-gather(bf16[4,6,128]{2,1,0:T(8,128)(2,1)S(1)} %all-to-all-done.1), channel_id=1, replica_groups=mesh['region'=4,'col'=8] {'col'}, dimensions={0}, use_global_device_ids=true | all-gather | bytes 55296 | tf_op jit(solution)/shard_map/all_gather | solution.py:72
  53.8 43.1 %add_convert_fusion = bf16[192,8,256,8]{3,2,1,0:T(8,128)(2,1)} fusion(f32[192,8,8]{2,1,0:T(8,128)S(1)} %get-tuple-element.34, f32[192,256]{1,0:T(8,128)S(1)} %get-tuple-element.38, f32[192,8,8]{2,1,0:T(8,128)S(1)} %get-tuple-element.33, f32[192,256]{1,0:T(8,128)S(1)} %get-tuple-element.37), kind=kLoop, calls=%fused_computation | loop fusion | flops 12582912 | bytes 6782976 | tf_op jit(solution)/shard_map/convert_element_type | solution.py:33
  96.9 141.8 %convert_element_type.99 = bf16[1536,2048]{1,0:T(8,128)(2,1)} reshape(bf16[192,8,256,8]{3,2,1,0:T(8,128)(2,1)} %add_convert_fusion) | data formatting | bytes 12582912 | tf_op jit(solution)/shard_map/convert_element_type | solution.py:33
  238.7 23.6 %add_convert_fusion.1 = bf16[192,8,128,8]{3,2,1,0:T(8,128)(2,1)} fusion(f32[192,8,8]{2,1,0:T(8,128)S(1)} %get-tuple-element.34, f32[192,128]{1,0:T(8,128)S(1)} %copy-done.9, f32[192,8,8]{2,1,0:T(8,128)S(1)} %get-tuple-element.33, f32[192,128]{1,0:T(8,128)S(1)} %copy-done.8), kind=kLoop, calls=%fused_computation.1 | loop fusion | flops 6291456 | bytes 3440640 | tf_op jit(solution)/shard_map/convert_element_type | solution.py:33
  262.3 71.0 %convert_element_type.103 = bf16[1536,1024]{1,0:T(8,128)(2,1)S(1)} reshape(bf16[192,8,128,8]{3,2,1,0:T(8,128)(2,1)} %add_convert_fusion.1) | data formatting | bytes 6291456 | tf_op jit(solution)/shard_map/convert_element_type | solution.py:33
  333.3 9.5 %select_add_fusion = f32[2048,1024]{0,1:T(8,128)S(1)} fusion(f32[2048]{0:T(1024)S(1)} %copy-done.10, s32[2048]{0:T(1024)S(1)} %iota_add_fusion, s32[1024]{0:T(1024)S(1)} %iota_add_fusion.1, bf16[1536,2048]{1,0:T(8,128)(2,1)} %convert_element_type.99, bf16[1536,1024]{1,0:T(8,128)(2,1)S(1)} %convert_element_type.103), kind=kOutput, calls=%fused_computation.2 | convolution fusion | flops 6448742400 | bytes 17846272 | tf_op jit(solution)/shard_map/dot_general | solution.py:81
  342.8 3.4 copy-done.3
  347.1 58.0 %all-reduce.3.cloned.1.call-done = bf16[2048,128]{0,1:T(8,128)(2,1)} async-done(((bf16[2048,128]{0,1:T(8,128)(2,1)}), bf16[2048,128]{0,1:T(8,128)(2,1)}) %all-reduce.3.cloned.1.call-update) | async-done | bytes 524304 | tf_op jit(solution)/shard_map/psum | solution.py:24
  407.9 9.7 %collective-permute-done = bf16[2048,128]{0,1:T(8,128)(2,1)S(1)} collective-permute-done((bf16[2048,128]{0,1:T(8,128)(2,1)}, bf16[2048,128]{0,1:T(8,128)(2,1)S(1)}, u32[]{:S(2)}, u32[]{:S(2)}) %collective-permute-start) | collective-permute-done | bytes 524320 | tf_op jit(solution)/shard_map/ppermute | solution.py:15
  421.0 20.1 %collective-permute-done.1 = bf16[4096,128]{0,1:T(8,128)(2,1)S(1)} collective-permute-done((bf16[4096,128]{0,1:T(8,128)(2,1)S(1)}, bf16[4096,128]{0,1:T(8,128)(2,1)S(1)}, u32[]{:S(2)}, u32[]{:S(2)}) %collective-permute-start.1) | collective-permute-done | bytes 1048608 | tf_op jit(solution)/shard_map/ppermute | solution.py:15
  447.1 11.7 %cholesky.44 = f32[128,128]{1,0:T(8,128)S(1)} custom-call(f32[128,128]{1,0:T(8,128)S(1)} %fusion.37), custom_call_target="Cholesky" | custom-call | tf_op jit(solution)/shard_map/jit(cholesky)/cholesky | solution.py:103
  460.2 9.8 %custom-call.10 = f32[1,128,128]{1,2,0:T(8,128)S(1)} custom-call(f32[1,128,128]{2,1,0:T(8,128)S(1)} %fusion.30), custom_call_target="InvertDiagBlocksLowerTriangular" | custom-call | tf_op jit(solution)/shard_map/jit(_solve_triangular)/triangular_solve | solution.py:107
  472.8 9.2 %convolution_subtract_fusion.1 = f32[2048,1024]{0,1:T(8,128)S(1)} fusion(f32[2048,1024]{0,1:T(8,128)} %copy-done.3, f32[2048,128]{0,1:T(8,128)S(1)} %fusion.1, f32[1024,128]{0,1:T(8,128)S(1)} %fusion.15), kind=kOutput, calls=%fused_computation.6 | convolution fusion | flops 3223322624 | bytes 18350080 | tf_op jit(solution)/shard_map/dot_general | solution.py:113
  488.1 58.6 %all-reduce.5.cloned.1.call-done = bf16[2048,128]{0,1:T(8,128)(2,1)} async-done(((bf16[2048,128]{0,1:T(8,128)(2,1)}), bf16[2048,128]{0,1:T(8,128)(2,1)}) %all-reduce.5.cloned.1.call-update) | async-done | bytes 524304 | tf_op jit(solution)/shard_map/psum | solution.py:24
  549.1 9.7 %collective-permute-done.2 = bf16[2048,128]{0,1:T(8,128)(2,1)S(1)} collective-permute-done((bf16[2048,128]{0,1:T(8,128)(2,1)}, bf16[2048,128]{0,1:T(8,128)(2,1)S(1)}, u32[]{:S(2)}, u32[]{:S(2)}) %collective-permute-start.2) | collective-permute-done | bytes 524320 | tf_op jit(solution)/shard_map/ppermute | solution.py:15
  562.3 19.9 %collective-permute-done.3 = bf16[4096,128]{0,1:T(8,128)(2,1)S(1)} collective-permute-done((bf16[4096,128]{0,1:T(8,128)(2,1)S(1)}, bf16[4096,128]{0,1:T(8,128)(2,1)S(1)}, u32[]{:S(2)}, u32[]{:S(2)}) %collective-permute-start.3) | collective-permute-done | bytes 1048608 | tf_op jit(solution)/shard_map/ppermute | solution.py:15
  588.2 11.7 %cholesky.55 = f32[128,128]{1,0:T(8,128)S(1)} custom-call(f32[128,128]{1,0:T(8,128)S(1)} %fusion.34), custom_call_target="Cholesky" | custom-call | tf_op jit(solution)/shard_map/jit(cholesky)/cholesky | solution.py:103
  601.3 9.8 %custom-call.12 = f32[1,128,128]{1,2,0:T(8,128)S(1)} custom-call(f32[1,128,128]{2,1,0:T(8,128)S(1)} %fusion.31), custom_call_target="InvertDiagBlocksLowerTriangular" | custom-call | tf_op jit(solution)/shard_map/jit(_solve_triangular)/triangular_solve | solution.py:107
  613.9 9.4 %convolution_subtract_fusion = f32[2048,1024]{0,1:T(8,128)S(1)} fusion(f32[2048,1024]{0,1:T(8,128)} %copy-done.2, f32[2048,128]{0,1:T(8,128)S(1)} %fusion, f32[1024,128]{0,1:T(8,128)S(1)} %fusion.14), kind=kOutput, calls=%fused_computation.5 | convolution fusion | flops 3223322624 | bytes 18350080 | tf_op jit(solution)/shard_map/dot_general | solution.py:113
  624.2 4.1 and_select_fusion.1
  628.4 9.3 %copy.43 = f32[2048,1024]{1,0:T(8,128)} copy(f32[2048,1024]{0,1:T(8,128)} %and_select_fusion.1) | data formatting | bytes 16777216 | tf_op jit(solution)/shard_map/jit(_where)/select_n | solution.py:118
  (95 shorter events, 50.1 us)
Async XLA Ops:
  6.5 8.7 %copy-start = (bf16[8,128]{1,0:T(8,128)(2,1)S(1)}, bf16[8,128]{1,0:T(8,128)(2,1)}, u32[]{:S(2)}) copy-start(bf16[8,128]{1,0:T(8,128)(2,1)} %param.15) | copy-start | bytes 6148
  10.1 9.9 %all-to-all-start = ((bf16[4,6,6]{1,2,0:T(8,128)(2,1)}), bf16[4,6,6]{1,2,0:T(8,128)(2,1)S(1)}, u32[]{:S(2)}, u32[]{:S(2)}) async-start(bf16[4,6,6]{1,2,0:T(8,128)(2,1)} %copy.34), calls=%async_computation | async-start | bytes 16384 | tf_op jit(solution)/shard_map/all_to_all | solution.py:70
  19.9 19.0 %all-to-all-start.1 = ((bf16[4,6,128]{2,1,0:T(8,128)(2,1)}), bf16[4,6,128]{2,1,0:T(8,128)(2,1)S(1)}, u32[]{:S(2)}, u32[]{:S(2)}) async-start(bf16[4,6,128]{2,1,0:T(8,128)(2,1)} %reshape.292), calls=%async_computation.1 | async-start | bytes 16384 | tf_op jit(solution)/shard_map/all_to_all | solution.py:69
  23.2 381.9 %all-reduce.3.cloned.1.call-start = ((), (), s32[]{:S(2)}) async-start(), calls=%async_computation.2 | async-start | bytes 1048576 | tf_op jit(solution)/shard_map/psum | solution.py:24
  96.9 141.8 %copy-start.8 = (f32[192,128]{1,0:T(8,128)S(1)}, f32[192,128]{1,0:T(8,128)}, u32[]{:S(2)}) copy-start(f32[192,128]{1,0:T(8,128)} %get-tuple-element.41) | copy-start | bytes 294916
  96.9 141.8 %copy-start.9 = (f32[192,128]{1,0:T(8,128)S(1)}, f32[192,128]{1,0:T(8,128)}, u32[]{:S(2)}) copy-start(f32[192,128]{1,0:T(8,128)} %get-tuple-element.42) | copy-start | bytes 294916
  262.3 71.0 %copy-start.10 = (f32[2048]{0:T(1024)S(1)}, f32[2048]{0:T(1024)}, u32[]{:S(2)}) copy-start(f32[2048]{0:T(1024)} %param.18) | copy-start | bytes 24580
  342.8 3.4 copy-start.3
  347.1 199.6 %all-reduce.5.cloned.1.call-start = ((), (), s32[]{:S(2)}) async-start(), calls=%async_computation.3 | async-start | bytes 1048576 | tf_op jit(solution)/shard_map/psum | solution.py:24
  405.1 12.5 %collective-permute-start = (bf16[2048,128]{0,1:T(8,128)(2,1)}, bf16[2048,128]{0,1:T(8,128)(2,1)S(1)}, u32[]{:S(2)}, u32[]{:S(2)}) collective-permute-start(bf16[2048,128]{0,1:T(8,128)(2,1)} %all-reduce.3.cloned.1.call-done), channel_id=1, source_target_pairs={{0,24},{8,0},{16,8},{24,16},{1,25},{9,1},{17,9},{25,17},{2,26},{10... | collective-permute-start | bytes 1572872 | tf_op jit(solution)/shard_map/ppermute | solution.py:15
  418.8 52.9 %copy-start.6 = (bf16[2048,128]{0,1:T(8,128)(2,1)S(1)}, bf16[2048,128]{0,1:T(8,128)(2,1)}, u32[]{:S(2)}) copy-start(bf16[2048,128]{0,1:T(8,128)(2,1)} %all-reduce.3.cloned.1.call-done) | copy-start | bytes 1572868
  418.8 22.3 %collective-permute-start.1 = (bf16[4096,128]{0,1:T(8,128)(2,1)S(1)}, bf16[4096,128]{0,1:T(8,128)(2,1)S(1)}, u32[]{:S(2)}, u32[]{:S(2)}) collective-permute-start(bf16[4096,128]{0,1:T(8,128)(2,1)S(1)} %pad_maximum_fusion), channel_id=1, source_target_pairs={{0,16},{8,24},{16,0},{24,8},{1,17},{9,25},{17,1},{25,9},{2,18},{10... | collective-permute-start | bytes 3145736 | tf_op jit(solution)/shard_map/ppermute | solution.py:15
  444.2 1.9 copy-start.5
  483.8 3.4 copy-start.2
  546.7 12.1 %collective-permute-start.2 = (bf16[2048,128]{0,1:T(8,128)(2,1)}, bf16[2048,128]{0,1:T(8,128)(2,1)S(1)}, u32[]{:S(2)}, u32[]{:S(2)}) collective-permute-start(bf16[2048,128]{0,1:T(8,128)(2,1)} %all-reduce.5.cloned.1.call-done), channel_id=1, source_target_pairs={{0,24},{8,0},{16,8},{24,16},{1,25},{9,1},{17,9},{25,17},{2,26},{10... | collective-permute-start | bytes 1572872 | tf_op jit(solution)/shard_map/ppermute | solution.py:15
  559.9 52.9 %copy-start.7 = (bf16[2048,128]{0,1:T(8,128)(2,1)S(1)}, bf16[2048,128]{0,1:T(8,128)(2,1)}, u32[]{:S(2)}) copy-start(bf16[2048,128]{0,1:T(8,128)(2,1)} %all-reduce.5.cloned.1.call-done) | copy-start | bytes 1572868
  559.9 22.3 %collective-permute-start.3 = (bf16[4096,128]{0,1:T(8,128)(2,1)S(1)}, bf16[4096,128]{0,1:T(8,128)(2,1)S(1)}, u32[]{:S(2)}, u32[]{:S(2)}) collective-permute-start(bf16[4096,128]{0,1:T(8,128)(2,1)S(1)} %pad_maximum_fusion.1), channel_id=1, source_target_pairs={{0,16},{8,24},{16,0},{24,8},{1,17},{9,25},{17,1},{25,9},{2,18},{10... | collective-permute-start | bytes 3145736 | tf_op jit(solution)/shard_map/ppermute | solution.py:15
  585.3 1.9 copy-start.4
  628.3 9.3 %copy-start.1 = (bf16[8,128]{1,0:T(8,128)(2,1)S(1)}, bf16[8,128]{1,0:T(8,128)(2,1)}, u32[]{:S(2)}) copy-start(bf16[8,128]{1,0:T(8,128)(2,1)} %param.15) | copy-start | bytes 6148
Sparse Core Ops, SparseCore 0:
  347.2 57.8 all-reduce.2
  488.2 58.4 all-reduce.4
